TPU v7x, 512 devices: a whole 4x4x16 slice. The times are simulated.
512 devices in a mesh: seq: 64 (over z, y), tp: 8 (over x, core).
Axes of the slice: x: 4, y: 4, z: 16, core: 2. Of those that a mesh axis runs over, the one named last changes fastest.
Arguments:
- hidden: bfloat16 [384, 2048], P(None, 'seq'), may hold values from -12 to 12
- ln1_gain: float32 [2048], P('seq'), may hold values from 0.1 to 1.9
- wq: bfloat16 [2048, 2048], P('seq', 'tp'), may hold values from -0.125 to 0.125
- wk: bfloat16 [2048, 1024], P('seq', 'tp'), may hold values from -0.125 to 0.125
- wv: bfloat16 [2048, 1024], P('seq', 'tp'), may hold values from -0.125 to 0.125
- wg: bfloat16 [2048, 2048], P('seq', 'tp'), may hold values from -0.125 to 0.125
- q_gain: float32 [128], replicated, may hold values from 1 to 30
- key_gain: float32 [128], replicated, may hold values from 0.5 to 1.5
- wo: bfloat16 [2048, 2048], P('tp', 'seq'), may hold values from -0.5 to 0.5
- ln2_gain: float32 [2048], P('seq'), may hold values from 0.1 to 1.9
- w_gate: bfloat16 [2048, 6144], P('seq', 'tp'), may hold values from -0.125 to 0.125
- w_up: bfloat16 [2048, 6144], P('seq', 'tp'), may hold values from -0.125 to 0.125
- w_down: bfloat16 [6144, 2048], P('tp', 'seq'), may hold values from -0.078125 to 0.078125
- last_gain: float32 [2048], P('seq'), may hold values from 0.1 to 1.9
- head_weight: bfloat16 [2048, 131072], P(None, ('seq', 'tp')), may hold values from -0.125 to 0.125
- inv_temp: float32 [8], replicated, may hold values from 0.5 to 64
- key_cache: bfloat16 [8, 16384, 1024], P(None, 'seq', 'tp'), may hold values from -40 to 40
- value_cache: bfloat16 [8, 16384, 1024], P(None, 'seq', 'tp'), may hold values from -6 to 6
- lengths: int32 [8], replicated, may hold values from 1 to 16336
- parents: int32 [8, 48], replicated, may hold values from 0 to 46, as said below
- accepted: int32 [8], replicated, may hold values from 0 to 47
Outputs:
- logprobs: float32 [384, 131072], P(None, ('seq', 'tp'))
- next_hidden: bfloat16 [384, 2048], P(None, 'seq')
- updated_key_cache: bfloat16 [8, 16384, 1024], P(None, 'seq', 'tp')
- updated_value_cache: bfloat16 [8, 16384, 1024], P(None, 'seq', 'tp')
Inputs may be any that keep to these rules, and one draw needn't show every extreme that they name: parents[r, 0] = 0; for i >= 1, i - 4 <= parents[r, i] < i.
All inputs are finite; a program needn't handle non-finite values.
Results may differ from a plain program's by a relative error of at most 0.012.
Values may be sent and summed in bfloat16 or wider, within the bound.
No kernel may reach another device: no remote copies, remote signals or barrier semaphores. Data moves between devices by JAX's collectives and lax.ppermute only.
A program may use at most 128 MiB of HBM per device.

v0:
```python
import jax
import jax.numpy as jnp
from jax import lax
from jax.sharding import Mesh, PartitionSpec as P

EPSILON = 1e-06
ROPE_BASE = 1000000.0
NEGATIVE = -1e30
BF = jnp.bfloat16
F32 = jnp.float32


def ancestry(parents):
    node_count = parents.shape[-1]
    node_ids = jnp.arange(node_count, dtype=jnp.int32)
    reachable = (parents[..., :, None] == node_ids[None, :]).astype(BF)
    reachable = jnp.maximum(reachable, jnp.eye(node_count, dtype=BF))
    for turn in range((node_count - 1).bit_length()):
        reachable = jnp.minimum(
            jnp.einsum("rij,rjk->rik", reachable, reachable, preferred_element_type=F32), 1.0
        ).astype(BF)
    return reachable.astype(F32)


def head_norm(values, gain):
    meansq = jnp.mean(values * values, axis=-1, keepdims=True)
    return values * lax.rsqrt(meansq + EPSILON) * gain


def rotate(values, cosine, sine):
    half = values.shape[-1] // 2
    low, high = (values[..., :half], values[..., half:])
    return jnp.concatenate([low * cosine - high * sine, high * cosine + low * sine], axis=-1)


def swap(values, axis):
    return lax.all_to_all(values, axis, 0, 0, tiled=True)


def spread(values, axis, count):
    return swap(jnp.broadcast_to(values[None], (count,) + values.shape), axis)


def split2(values):
    high = values.astype(BF)
    low = (values - high.astype(F32)).astype(BF)
    return (high, low)


def split3(values):
    high = values.astype(BF)
    rest = values - high.astype(F32)
    mid = rest.astype(BF)
    low = (rest - mid.astype(F32)).astype(BF)
    return (high, mid, low)


def pack_state(peak, mass, weighted):
    count = peak.shape[0]
    mass_high, mass_low = split2(mass)
    stats = jnp.stack([peak.astype(BF), mass_high, mass_low], axis=1).reshape(count, 6, 24)
    stats = jnp.pad(stats, ((0, 0), (0, 2), (0, 104)))
    return jnp.concatenate([weighted.astype(BF).reshape(count, 48, 128), stats], axis=1)


def merge_state(packed):
    count = packed.shape[0]
    weighted = packed[:, :48].reshape(count, 2, 24, 128).astype(F32)
    stats = packed[:, 48:54, :24].astype(F32).reshape(count, 3, 2, 24)
    peaks, masses = (stats[:, 0], stats[:, 1] + stats[:, 2])
    peak = jnp.max(peaks, axis=0)
    factor = jnp.exp(peaks - peak)
    return (peak, jnp.sum(masses * factor, axis=0), jnp.sum(weighted * factor[..., None], axis=0))


def on_device(
    hidden,
    ln1_gain,
    wq,
    wk,
    wv,
    wg,
    q_gain,
    key_gain,
    wo,
    ln2_gain,
    w_gate,
    w_up,
    w_down,
    last_gain,
    head_weight,
    inv_temp,
    key_cache,
    value_cache,
    lengths,
    parents,
    accepted,
):
    z, y, x, c = (lax.axis_index(name) for name in ("z", "y", "x", "c"))
    seq = z * 4 + y
    requests, tree = parents.shape
    slot_count = key_cache.shape[1]
    width = 2048
    token = jnp.arange(384, dtype=jnp.int32)
    token_y = token // 6 % 4
    place = token_y * 128 + token // 24 * 6 + token % 6
    scatter = (place[:, None] == jnp.arange(512, dtype=jnp.int32)[None, :]).astype(BF)
    hidden_t = jnp.dot(hidden.T, scatter, preferred_element_type=F32).astype(BF)
    gains = jnp.stack(split3(ln1_gain) + split3(ln2_gain) + split3(last_gain), axis=1)
    gains = jnp.pad(gains, ((0, 0), (96, 128 - 96 - 9)))
    down_t, wo_t = (w_down.T, wo.T)
    pieces = []
    for part in range(4):
        pieces.append(
            jnp.concatenate(
                [
                    w_gate[:, part * 192 : part * 192 + 192],
                    w_up[:, part * 192 : part * 192 + 192],
                    down_t[:, part * 192 : part * 192 + 192],
                    wo_t[:, part * 64 : part * 64 + 64],
                    wq,
                    wk,
                    wv,
                    wg,
                    hidden_t[:, part * 128 : part * 128 + 128] + gains,
                ],
                axis=1,
            )
        )
    mine = swap(jnp.stack(pieces), "y").reshape(128, 1536)
    ffn = lax.all_gather(mine[:, :640], "z", axis=0, tiled=True)
    proj = mine[:, 640:1408]
    side = mine[:, 1408:]
    side_wide = side.astype(F32)
    ln1_row = side_wide[:, 96:97] + side_wide[:, 97:98] + side_wide[:, 98:99]
    scaled = (side_wide * ln1_row).astype(BF)
    partial = lax.dot_general(scaled, proj, (((0,), (0,)), ((), ())), preferred_element_type=F32)
    sent = jnp.concatenate([partial[:96].astype(BF), side.T[:96]], axis=1).reshape(16, 6, 896)
    got = swap(sent, "z")
    sums = jnp.sum(got[:, :, :768].astype(F32), axis=0)
    rows = got[:, :, 768:]
    rows_wide = rows.astype(F32)
    squares = jnp.sum(rows_wide * rows_wide, axis=(0, 2))
    sums = sums * lax.rsqrt(squares / width + EPSILON)[:, None]
    links = ancestry(parents)
    depth = jnp.sum((links > 0.5).astype(jnp.int32), axis=-1) - 1
    target = lengths[:, None] + depth
    my_places = lax.dynamic_slice(target.reshape(-1), (z * 24 + y * 6,), (6,))
    inverse = ROPE_BASE ** (-jnp.arange(64, dtype=F32) / 64)
    angles = my_places.astype(F32)[:, None] * inverse[None, :]
    cosine, sine = (jnp.cos(angles)[:, None, :], jnp.sin(angles)[:, None, :])
    query = rotate(head_norm(sums[:, :256].reshape(6, 2, 128), q_gain), cosine, sine) * 128 ** (
        -0.5
    )
    new_key = rotate(head_norm(sums[:, 256:384].reshape(6, 1, 128), key_gain), cosine, sine)
    outgate = jax.nn.sigmoid(sums[:, 512:])
    mine6 = jnp.concatenate(
        [query.reshape(6, 256), new_key.reshape(6, 128), sums[:, 384:512], outgate], axis=1
    ).astype(BF)
    gain_row = side[:, 99:105].T.reshape(1, 768)
    block = jnp.concatenate([mine6, gain_row, jnp.zeros((1, 768), BF)], axis=0)
    gathered = spread(block, "z", 16)
    gain_all = gathered[:, 6].reshape(16, 6, 128).astype(F32)
    ln2_all = gain_all[:, 0] + gain_all[:, 1] + gain_all[:, 2]
    last_all = gain_all[:, 3] + gain_all[:, 4] + gain_all[:, 5]
    tokens = spread(gathered[:, :6].reshape(96, 768), "y", 4).reshape(384, 768)
    order = token_y * 96 + token // 24 * 6 + token % 6
    gather = (order[:, None] == token[None, :]).astype(BF)
    tokens = jnp.dot(gather, tokens, preferred_element_type=F32).astype(BF)
    queries = tokens[:, :256].reshape(requests, tree, 2, 128)
    tree_keys = tokens[:, 256:384].reshape(requests, tree, 128)
    tree_values = tokens[:, 384:512].reshape(requests, tree, 128)
    gates = tokens[:, 512:]
    slot_ids = seq * slot_count + jnp.arange(slot_count, dtype=jnp.int32)
    valid_slot = (slot_ids[None, :] < lengths[:, None])[:, None, None, :]
    valid_node = ((links > 0.5) & (seq == 0))[:, None, :, :]
    scores = jnp.einsum("rigd,rcd->rgic", queries, key_cache, preferred_element_type=F32)
    tree_scores = jnp.einsum("rigd,rjd->rgij", queries, tree_keys, preferred_element_type=F32)
    peak = jnp.maximum(
        jnp.max(jnp.where(valid_slot, scores, NEGATIVE), axis=-1),
        jnp.max(jnp.where(valid_node, tree_scores, NEGATIVE), axis=-1),
    )
    peak = lax.reduce_precision(peak, 8, 7)
    weights = jnp.where(valid_slot, jnp.exp(scores - peak[..., None]), 0.0)
    tree_weights = jnp.where(valid_node, jnp.exp(tree_scores - peak[..., None]), 0.0)
    mass = jnp.sum(weights, axis=-1) + jnp.sum(tree_weights, axis=-1)
    weighted = jnp.einsum(
        "rgic,rcd->rgid", weights.astype(BF), value_cache, preferred_element_type=F32
    ) + jnp.einsum(
        "rgij,rjd->rgid", tree_weights.astype(BF), tree_values, preferred_element_type=F32
    )

    def by_z(values):
        split = values.reshape((requests, 2, 2, 24) + values.shape[3:])
        return jnp.swapaxes(split, 1, 2).reshape((16, 2, 24) + values.shape[3:])

    state = merge_state(swap(pack_state(by_z(peak), by_z(mass), by_z(weighted)), "z"))
    packed = pack_state(*(part[None] for part in state))[0]
    both = spread(jnp.concatenate([packed, rows.reshape(96, 128)], axis=0), "y", 4)
    peak, mass, weighted = merge_state(both[:, :56])
    my_gate = lax.dynamic_slice(gates, (z * 24, 0), (24, 256)).reshape(24, 2, 128)
    my_gate = jnp.swapaxes(my_gate, 0, 1).astype(F32)
    gated = (weighted / mass[..., None] * my_gate).astype(BF)
    gated = lax.dynamic_index_in_dim(gated, y // 2, 0, keepdims=False)
    gated = jnp.where(y % 2 == 0, gated[:, :64], gated[:, 64:])
    column = y * 4 + x
    hidden_mine = lax.dynamic_index_in_dim(
        both[:, 56:].reshape(4, 16, 6, 128), column, 1, keepdims=False
    ).reshape(24, 128)

    def reduce_columns(part):
        part = jnp.swapaxes(part.astype(BF).reshape(24, 16, 128), 0, 1)
        part = jnp.sum(swap(part, ("y", "x")).astype(F32), axis=0)
        return part + lax.ppermute(part, "c", [(0, 1), (1, 0)])

    attn = lax.dot_general(
        gated, ffn[:, 576:], (((1,), (1,)), ((), ())), preferred_element_type=F32
    )
    middle = (hidden_mine.astype(F32) + reduce_columns(attn)).astype(BF)
    middle_all = spread(middle, ("y", "x"), 16).astype(F32)
    squares_mid = jnp.sum(middle_all * middle_all, axis=(0, 2))
    scale_mid = lax.rsqrt(squares_mid / width + EPSILON)
    normed2 = (middle_all * scale_mid[None, :, None] * ln2_all[:, None, :]).astype(BF)
    normed2 = jnp.swapaxes(normed2, 0, 1).reshape(24, width)
    hidden_units = jnp.dot(normed2, ffn[:, :384], preferred_element_type=F32)
    activated = (jax.nn.silu(hidden_units[:, :192]) * hidden_units[:, 192:]).astype(BF)
    down = lax.dot_general(
        activated, ffn[:, 384:576], (((1,), (1,)), ((), ())), preferred_element_type=F32
    )
    following = (middle.astype(F32) + reduce_columns(down)).astype(BF)
    half = spread(following, "z", 16).reshape(384, 128)
    half = lax.dynamic_slice(half, (c * 192, 0), (192, 128))
    half = spread(spread(half, "y", 4), "x", 4)
    other = lax.ppermute(half, "c", [(0, 1), (1, 0)])
    full = jnp.stack([jnp.where(c == 0, half, other), jnp.where(c == 0, other, half)])
    own = lax.dynamic_slice(full, (0, z % 4, z // 4, 0, 0), (2, 1, 1, 192, 128)).reshape(384, 128)
    next_hidden = lax.dynamic_slice(own, (0, y * 32), (384, 32))
    full = jnp.transpose(full, (0, 3, 2, 1, 4)).reshape(384, width)
    wide = full.astype(F32)
    squares_last = jnp.sum(wide * wide, axis=1)
    normed3 = (
        wide * lax.rsqrt(squares_last / width + EPSILON)[:, None] * last_all.reshape(1, width)
    ).astype(BF)
    logits = jnp.dot(normed3, head_weight, preferred_element_type=F32)
    logits = logits * jnp.repeat(inv_temp, tree)[:, None]
    top = jnp.max(logits, axis=1)
    spot = top + jnp.log(jnp.sum(jnp.exp(logits - top[:, None]), axis=1))
    for axis, count in ((("y", "x", "c"), 32), ("z", 16)):
        spots = spread(spot.reshape(3, 128), axis, count)
        top = jnp.max(spots, axis=0)
        spot = top + jnp.log(jnp.sum(jnp.exp(spots - top), axis=0))
    logprobs = logits - spot.reshape(384, 1)
    accepted_rows = links[jnp.arange(requests), accepted]
    placed = (slot_ids[None, :, None] == target[:, None, :]).astype(F32) * accepted_rows[:, None, :]
    hits = (jnp.sum(placed, axis=2) > 0.5)[:, :, None]
    placed = placed.astype(BF)
    moved_keys = jnp.einsum("rca,rae->rce", placed, tree_keys, preferred_element_type=F32).astype(
        BF
    )
    moved_values = jnp.einsum(
        "rca,rae->rce", placed, tree_values, preferred_element_type=F32
    ).astype(BF)
    return (
        logprobs,
        next_hidden,
        jnp.where(hits, moved_keys, key_cache),
        jnp.where(hits, moved_values, value_cache),
    )


def solution(mesh):
    grid = Mesh(mesh.devices.reshape(16, 4, 4, 2), ("z", "y", "x", "c"))
    seq, tp = (("z", "y"), ("x", "c"))
    in_specs = (
        P(None, seq),
        P(seq),
        P(seq, tp),
        P(seq, tp),
        P(seq, tp),
        P(seq, tp),
        P(),
        P(),
        P(tp, seq),
        P(seq),
        P(seq, tp),
        P(seq, tp),
        P(tp, seq),
        P(seq),
        P(None, seq + tp),
        P(),
        P(None, seq, tp),
        P(None, seq, tp),
        P(),
        P(),
        P(),
    )
    out_specs = (P(None, seq + tp), P(None, seq), P(None, seq, tp), P(None, seq, tp))
    return jax.shard_map(
        on_device, mesh=grid, in_specs=in_specs, out_specs=out_specs, check_vma=False
    )
```

profile of v0, /device:TPU:1, one launch (start us, length us, event | category | flops | bytes accessed | tf_op | source)
XLA Modules:
  0.0 322.7 jit_solution(3381878387999184094)
XLA Ops:
  7.2 0.8 convert_bitcast_fusion.10
  8.3 0.7 convert_bitcast_fusion.7
  9.3 0.7 convert_bitcast_fusion.4
  10.4 0.9 fusion.142
  11.3 0.9 fusion.144
  12.1 1.0 fusion.19
  13.3 0.9 fusion.140
  14.3 0.9 concatenate.48
  15.1 0.9 concatenate.49
  16.0 0.9 concatenate.50
  16.9 0.9 concatenate.51
  17.7 0.8 pad_maximum_fusion.1
  18.5 5.0 %all-to-all-start = ((bf16[4,32,1536]{2,1,0:T(8,128)(2,1)}), bf16[4,32,1536]{2,1,0:T(8,128)(2,1)S(1)}, u32[]{:S(2)}, u32[]{:S(2)}) async-start(bf16[4,32,1536]{2,1,0:T(8,128)(2,1)} %pad_maximum_fusion.1), calls=%async_computation | async-start | bytes 786432 | tf_op jit(solution)/shard_map/all_to_all | solution.py:37
  24.5 1.1 fusion.72
  26.1 3.7 %all-to-all-done = bf16[4,32,1536]{2,1,0:T(8,128)(2,1)S(1)} async-done(((bf16[4,32,1536]{2,1,0:T(8,128)(2,1)}), bf16[4,32,1536]{2,1,0:T(8,128)(2,1)S(1)}, u32[]{:S(2)}, u32[]{:S(2)}) %all-to-all-start) | async-done | bytes 393248 | tf_op jit(solution)/shard_map/all_to_all | solution.py:37
  30.2 0.7 reshape.543
  30.9 15.6 %all-to-all-start.1 = ((bf16[16,6,896]{2,1,0:T(8,128)(2,1)}), bf16[16,6,896]{2,1,0:T(8,128)(2,1)S(1)}, u32[]{:S(2)}, u32[]{:S(2)}) async-start(bf16[16,6,896]{2,1,0:T(8,128)(2,1)} %reshape.543), calls=%async_computation.1 | async-start | bytes 458752 | tf_op jit(solution)/shard_map/all_to_all | solution.py:37
  46.9 12.2 %all-to-all-done.1 = bf16[16,6,896]{2,1,0:T(8,128)(2,1)S(1)} async-done(((bf16[16,6,896]{2,1,0:T(8,128)(2,1)}), bf16[16,6,896]{2,1,0:T(8,128)(2,1)S(1)}, u32[]{:S(2)}, u32[]{:S(2)}) %all-to-all-start.1) | async-done | bytes 172064 | tf_op jit(solution)/shard_map/all_to_all | solution.py:37
  60.2 0.7 broadcast_in_dim.72
  60.9 8.4 %all-to-all-start.2 = ((bf16[16,8,768]{2,1,0:T(8,128)(2,1)}), bf16[16,8,768]{2,1,0:T(8,128)(2,1)S(1)}, u32[]{:S(2)}, u32[]{:S(2)}) async-start(bf16[16,8,768]{2,1,0:T(8,128)(2,1)} %broadcast_in_dim.72), calls=%async_computation.2 | async-start | bytes 393216 | tf_op jit(solution)/shard_map/all_to_all | solution.py:37
  69.6 12.1 %all-to-all-done.2 = bf16[16,8,768]{2,1,0:T(8,128)(2,1)S(1)} async-done(((bf16[16,8,768]{2,1,0:T(8,128)(2,1)}), bf16[16,8,768]{2,1,0:T(8,128)(2,1)S(1)}, u32[]{:S(2)}, u32[]{:S(2)}) %all-to-all-start.2) | async-done | bytes 196640 | tf_op jit(solution)/shard_map/all_to_all | solution.py:37
  81.8 0.9 broadcast_in_dim.74
  82.6 3.6 %all-to-all-start.3 = ((bf16[4,96,768]{2,1,0:T(8,128)(2,1)}), bf16[4,96,768]{2,1,0:T(8,128)(2,1)S(1)}, u32[]{:S(2)}, u32[]{:S(2)}) async-start(bf16[4,96,768]{2,1,0:T(8,128)(2,1)} %broadcast_in_dim.74), calls=%async_computation.3 | async-start | bytes 1179648 | tf_op jit(solution)/shard_map/all_to_all | solution.py:37
  87.1 6.4 %all-to-all-done.3 = bf16[4,96,768]{2,1,0:T(8,128)(2,1)S(1)} async-done(((bf16[4,96,768]{2,1,0:T(8,128)(2,1)}), bf16[4,96,768]{2,1,0:T(8,128)(2,1)S(1)}, u32[]{:S(2)}, u32[]{:S(2)}) %all-to-all-start.3) | async-done | bytes 589856 | tf_op jit(solution)/shard_map/all_to_all | solution.py:37
  96.4 0.7 fusion.36
  97.1 7.2 %all-to-all-start.4 = ((bf16[16,56,128]{2,1,0:T(8,128)(2,1)}), bf16[16,56,128]{2,1,0:T(8,128)(2,1)S(1)}, u32[]{:S(2)}, u32[]{:S(2)}) async-start(bf16[16,56,128]{2,1,0:T(8,128)(2,1)} %fusion.36), calls=%async_computation.4 | async-start | bytes 458752 | tf_op jit(solution)/shard_map/all_to_all | solution.py:37
  104.4 13.2 %all-to-all-done.4 = bf16[16,56,128]{2,1,0:T(8,128)(2,1)S(1)} async-done(((bf16[16,56,128]{2,1,0:T(8,128)(2,1)}), bf16[16,56,128]{2,1,0:T(8,128)(2,1)S(1)}, u32[]{:S(2)}, u32[]{:S(2)}) %all-to-all-start.4) | async-done | bytes 229408 | tf_op jit(solution)/shard_map/all_to_all | solution.py:37
  118.2 0.7 broadcast_in_dim.80
  118.9 3.3 %all-to-all-start.5 = ((bf16[4,152,128]{2,1,0:T(8,128)(2,1)}), bf16[4,152,128]{2,1,0:T(8,128)(2,1)S(1)}, u32[]{:S(2)}, u32[]{:S(2)}) async-start(bf16[4,152,128]{2,1,0:T(8,128)(2,1)} %broadcast_in_dim.80), calls=%async_computation.5 | async-start | bytes 311296 | tf_op jit(solution)/shard_map/all_to_all | solution.py:37
  122.3 4.9 %all-to-all-done.5 = bf16[4,152,128]{2,1,0:T(8,128)(2,1)S(1)} async-done(((bf16[4,152,128]{2,1,0:T(8,128)(2,1)}), bf16[4,152,128]{2,1,0:T(8,128)(2,1)S(1)}, u32[]{:S(2)}, u32[]{:S(2)}) %all-to-all-start.5) | async-done | bytes 155680 | tf_op jit(solution)/shard_map/all_to_all | solution.py:37
  127.6 34.2 %all-gather.2.cloned.1.call-done = bf16[2048,640]{1,0:T(8,128)(2,1)} async-done(((bf16[128,640]{1,0:T(8,128)(2,1)}), bf16[2048,640]{1,0:T(8,128)(2,1)}) %all-gather.2.cloned.1.call-update) | async-done | bytes 2621456 | tf_op jit(solution)/shard_map/all_gather | solution.py:131
  161.8 1.4 fusion.17
  163.8 5.8 %all-to-all-start.6 = ((bf16[16,24,128]{2,1,0:T(8,128)(2,1)}), bf16[16,24,128]{2,1,0:T(8,128)(2,1)S(1)}, u32[]{:S(2)}, u32[]{:S(2)}) async-start(bf16[16,24,128]{2,1,0:T(8,128)(2,1)} %bitcast.189), calls=%async_computation.6 | async-start | bytes 196608 | tf_op jit(solution)/shard_map/all_to_all | solution.py:37
  169.9 6.4 %all-to-all-done.6 = bf16[16,24,128]{2,1,0:T(8,128)(2,1)S(1)} async-done(((bf16[16,24,128]{2,1,0:T(8,128)(2,1)}), bf16[16,24,128]{2,1,0:T(8,128)(2,1)S(1)}, u32[]{:S(2)}, u32[]{:S(2)}) %all-to-all-start.6) | async-done | bytes 98336 | tf_op jit(solution)/shard_map/all_to_all | solution.py:37
  176.3 12.0 %collective-permute-start = (f32[24,128]{1,0:T(8,128)S(1)}, f32[24,128]{1,0:T(8,128)S(1)}, u32[]{:S(2)}, u32[]{:S(2)}) collective-permute-start(f32[24,128]{1,0:T(8,128)S(1)} %convert_reduce_fusion.2), channel_id=1, source_target_pairs={{0,1},{1,0},{2,3},{3,2},{4,5},{5,4},{6,7},{7,6},{8,9},{9,8},{10,11... | collective-permute-start | bytes 36872 | tf_op jit(solution)/shard_map/ppermute | solution.py:214
  188.4 0.8 collective-permute-done
  189.8 3.5 %all-to-all-start.7 = ((bf16[16,24,128]{2,1,0:T(8,128)(2,1)}), bf16[16,24,128]{2,1,0:T(8,128)(2,1)S(1)}, u32[]{:S(2)}, u32[]{:S(2)}) async-start(bf16[16,24,128]{2,1,0:T(8,128)(2,1)} %broadcast_in_dim.81), calls=%async_computation.7 | async-start | bytes 196608 | tf_op jit(solution)/shard_map/all_to_all | solution.py:37
  193.4 6.6 %all-to-all-done.7 = bf16[16,24,128]{2,1,0:T(8,128)(2,1)S(1)} async-done(((bf16[16,24,128]{2,1,0:T(8,128)(2,1)}), bf16[16,24,128]{2,1,0:T(8,128)(2,1)S(1)}, u32[]{:S(2)}, u32[]{:S(2)}) %all-to-all-start.7) | async-done | bytes 98336 | tf_op jit(solution)/shard_map/all_to_all | solution.py:37
  200.1 1.8 fusion.2
  201.9 1.6 fusion.18
  203.5 9.8 %all_to_all.70 = bf16[16,24,128]{2,1,0:T(8,128)(2,1)S(1)} all-to-all(bf16[16,24,128]{2,1,0:T(8,128)(2,1)S(1)} %bitcast.208), channel_id=1, replica_groups=mesh['z'=16,'y'=4,'x'=4,'c'=2] {'y','x'}, dimensions={0} | all-to-all | bytes 196608 | tf_op jit(solution)/shard_map/all_to_all | solution.py:37
  213.4 4.5 %collective-permute-start.1 = (f32[24,128]{1,0:T(8,128)S(1)}, f32[24,128]{1,0:T(8,128)S(1)}, u32[]{:S(2)}, u32[]{:S(2)}) collective-permute-start(f32[24,128]{1,0:T(8,128)S(1)} %convert_reduce_fusion.1), channel_id=1, source_target_pairs={{0,1},{1,0},{2,3},{3,2},{4,5},{5,4},{6,7},{7,6},{8,9},{9,8},{10,11... | collective-permute-start | bytes 36872 | tf_op jit(solution)/shard_map/ppermute | solution.py:214
  217.9 0.8 collective-permute-done.1
  219.4 6.5 %all-to-all-start.9 = ((bf16[16,24,128]{2,1,0:T(8,128)(2,1)}), bf16[16,24,128]{2,1,0:T(8,128)(2,1)S(1)}, u32[]{:S(2)}, u32[]{:S(2)}) async-start(bf16[16,24,128]{2,1,0:T(8,128)(2,1)} %broadcast_in_dim.82), calls=%async_computation.9 | async-start | bytes 196608 | tf_op jit(solution)/shard_map/all_to_all | solution.py:37
  225.9 11.9 %all-to-all-done.9 = bf16[16,24,128]{2,1,0:T(8,128)(2,1)S(1)} async-done(((bf16[16,24,128]{2,1,0:T(8,128)(2,1)}), bf16[16,24,128]{2,1,0:T(8,128)(2,1)S(1)}, u32[]{:S(2)}, u32[]{:S(2)}) %all-to-all-start.9) | async-done | bytes 98336 | tf_op jit(solution)/shard_map/all_to_all | solution.py:37
  237.8 7.5 %all_to_all.71 = bf16[4,192,128]{2,1,0:T(8,128)(2,1)S(1)} all-to-all(bf16[4,192,128]{2,1,0:T(8,128)(2,1)S(1)} %broadcast_in_dim.83), channel_id=1, replica_groups=mesh['z'=16,'y'=4,'x'=4,'c'=2] {'y'}, dimensions={0} | all-to-all | bytes 393216 | tf_op jit(solution)/shard_map/all_to_all | solution.py:37
  245.3 1.0 broadcast_in_dim.84
  246.4 3.5 %all-to-all-start.11 = ((bf16[4,4,192,128]{3,2,1,0:T(8,128)(2,1)}), bf16[4,4,192,128]{3,2,1,0:T(8,128)(2,1)S(1)}, u32[]{:S(2)}, u32[]{:S(2)}) async-start(bf16[4,4,192,128]{3,2,1,0:T(8,128)(2,1)} %broadcast_in_dim.84), calls=%async_computation.11 | async-start | bytes 1572864 | tf_op jit(solution)/shard_map/all_to_all | solution.py:37
  249.9 1.5 gather_fusion
  251.4 6.8 %all-to-all-done.11 = bf16[4,4,192,128]{3,2,1,0:T(8,128)(2,1)S(1)} async-done(((bf16[4,4,192,128]{3,2,1,0:T(8,128)(2,1)}), bf16[4,4,192,128]{3,2,1,0:T(8,128)(2,1)S(1)}, u32[]{:S(2)}, u32[]{:S(2)}) %all-to-all-start.11) | async-done | bytes 786464 | tf_op jit(solution)/shard_map/all_to_all | solution.py:37
  258.2 7.0 %collective-permute-start.2 = (bf16[4,4,192,128]{3,2,1,0:T(8,128)(2,1)S(1)}, bf16[4,4,192,128]{3,2,1,0:T(8,128)(2,1)}, u32[]{:S(2)}, u32[]{:S(2)}) collective-permute-start(bf16[4,4,192,128]{3,2,1,0:T(8,128)(2,1)S(1)} %all-to-all-done.11), channel_id=1, source_target_pairs={{0,1},{1,0},{2,3},{3,2},{4,5},{5,4},{6,7},{7,6},{8,9},{9,8},{10,11... | collective-permute-start | bytes 2359304 | tf_op jit(solution)/shard_map/ppermute | solution.py:234
  265.6 1.7 fusion.6
  267.3 1.6 fusion.7
  268.9 1.2 select_bitcast_fusion.1
  270.5 1.9 convert_bitcast_fusion
  272.5 5.6 %copy.190 = f32[2,192,4,4,128]{4,3,2,1,0:T(4,128)} copy(f32[2,192,4,4,128]{4,1,2,3,0:T(8,128)} %convert_bitcast_fusion) | data formatting | bytes 6291456 | tf_op jit(solution)/shard_map/convert_element_type | solution.py:239
  278.1 5.1 %reshape.571 = f32[384,2048]{1,0:T(8,128)} reshape(f32[2,192,4,4,128]{4,3,2,1,0:T(4,128)} %copy.190) | data formatting | bytes 6291456 | tf_op jit(solution)/shard_map/convert_element_type | solution.py:239
  283.2 2.7 fusion.148
  286.7 3.6 %all-to-all-start.12 = ((f32[32,3,128]{2,1,0:T(4,128)}), f32[32,3,128]{2,1,0:T(4,128)S(1)}, u32[]{:S(2)}, u32[]{:S(2)}) async-start(f32[32,3,128]{2,1,0:T(4,128)} %broadcast_in_dim.86), calls=%async_computation.12 | async-start | bytes 131072 | tf_op jit(solution)/shard_map/all_to_all | solution.py:37
  290.4 7.3 %all-to-all-done.12 = f32[32,3,128]{2,1,0:T(4,128)S(1)} async-done(((f32[32,3,128]{2,1,0:T(4,128)}), f32[32,3,128]{2,1,0:T(4,128)S(1)}, u32[]{:S(2)}, u32[]{:S(2)}) %all-to-all-start.12) | async-done | bytes 49184 | tf_op jit(solution)/shard_map/all_to_all | solution.py:37
  298.4 4.9 %all-to-all-start.13 = ((f32[16,3,128]{2,1,0:T(4,128)}), f32[16,3,128]{2,1,0:T(4,128)S(1)}, u32[]{:S(2)}, u32[]{:S(2)}) async-start(f32[16,3,128]{2,1,0:T(4,128)} %broadcast_in_dim.87), calls=%async_computation.13 | async-start | bytes 65536 | tf_op jit(solution)/shard_map/all_to_all | solution.py:37
  303.4 0.7 copy.196
  304.1 10.7 %all-to-all-done.13 = f32[16,3,128]{2,1,0:T(4,128)S(1)} async-done(((f32[16,3,128]{2,1,0:T(4,128)}), f32[16,3,128]{2,1,0:T(4,128)S(1)}, u32[]{:S(2)}, u32[]{:S(2)}) %all-to-all-start.13) | async-done | bytes 24608 | tf_op jit(solution)/shard_map/all_to_all | solution.py:37
  314.9 0.9 copy.195
  (174 shorter events, 14.2 us)
Async XLA Ops:
  7.2 276.0 %copy-start = (bf16[2048,256]{1,0:T(8,128)(2,1)S(1)}, bf16[2048,256]{1,0:T(8,128)(2,1)}, u32[]{:S(2)}) copy-start(bf16[2048,256]{1,0:T(8,128)(2,1)} %param.35) | copy-start | bytes 3145732
  7.2 16.4 %copy-start.7 = (s32[8,48]{1,0:T(8,128)S(1)}, s32[8,48]{1,0:T(8,128)}, u32[]{:S(2)}) copy-start(s32[8,48]{1,0:T(8,128)} %param.40) | copy-start | bytes 4612
  7.2 18.6 %copy-start.3 = (s32[8]{0:T(128)S(1)}, s32[8]{0:T(128)}, u32[]{:S(2)}) copy-start(s32[8]{0:T(128)} %param.39) | copy-start | bytes 100
  17.7 41.9 %copy-start.4 = (f32[128]{0:T(128)S(1)}, f32[128]{0:T(128)}, u32[]{:S(2)}) copy-start(f32[128]{0:T(128)} %param.27) | copy-start | bytes 1540
  17.7 42.2 %copy-start.5 = (f32[128]{0:T(128)S(1)}, f32[128]{0:T(128)}, u32[]{:S(2)}) copy-start(f32[128]{0:T(128)} %param.28) | copy-start | bytes 1540
  18.5 11.2 %all-to-all-start = ((bf16[4,32,1536]{2,1,0:T(8,128)(2,1)}), bf16[4,32,1536]{2,1,0:T(8,128)(2,1)S(1)}, u32[]{:S(2)}, u32[]{:S(2)}) async-start(bf16[4,32,1536]{2,1,0:T(8,128)(2,1)} %pad_maximum_fusion.1), calls=%async_computation | async-start | bytes 786432 | tf_op jit(solution)/shard_map/all_to_all | solution.py:37
  30.9 28.2 %all-to-all-start.1 = ((bf16[16,6,896]{2,1,0:T(8,128)(2,1)}), bf16[16,6,896]{2,1,0:T(8,128)(2,1)S(1)}, u32[]{:S(2)}, u32[]{:S(2)}) async-start(bf16[16,6,896]{2,1,0:T(8,128)(2,1)} %reshape.543), calls=%async_computation.1 | async-start | bytes 458752 | tf_op jit(solution)/shard_map/all_to_all | solution.py:37
  60.9 20.8 %all-to-all-start.2 = ((bf16[16,8,768]{2,1,0:T(8,128)(2,1)}), bf16[16,8,768]{2,1,0:T(8,128)(2,1)S(1)}, u32[]{:S(2)}, u32[]{:S(2)}) async-start(bf16[16,8,768]{2,1,0:T(8,128)(2,1)} %broadcast_in_dim.72), calls=%async_computation.2 | async-start | bytes 393216 | tf_op jit(solution)/shard_map/all_to_all | solution.py:37
  82.6 11.9 %copy-start.1 = (bf16[8,256,128]{2,1,0:T(8,128)(2,1)S(1)}, bf16[8,256,128]{2,1,0:T(8,128)(2,1)}, u32[]{:S(2)}) copy-start(bf16[8,256,128]{2,1,0:T(8,128)(2,1)} %param.37) | copy-start | bytes 1572868
  82.6 10.9 %all-to-all-start.3 = ((bf16[4,96,768]{2,1,0:T(8,128)(2,1)}), bf16[4,96,768]{2,1,0:T(8,128)(2,1)S(1)}, u32[]{:S(2)}, u32[]{:S(2)}) async-start(bf16[4,96,768]{2,1,0:T(8,128)(2,1)} %broadcast_in_dim.74), calls=%async_computation.3 | async-start | bytes 1179648 | tf_op jit(solution)/shard_map/all_to_all | solution.py:37
  86.2 75.6 %all-gather.2.cloned.1.call-start = ((), (), s32[]{:S(2)}) async-start(), calls=%async_computation.14 | async-start | bytes 2785280 | tf_op jit(solution)/shard_map/all_gather | solution.py:131
  94.0 1.7 copy-start.2
  97.1 20.5 %all-to-all-start.4 = ((bf16[16,56,128]{2,1,0:T(8,128)(2,1)}), bf16[16,56,128]{2,1,0:T(8,128)(2,1)S(1)}, u32[]{:S(2)}, u32[]{:S(2)}) async-start(bf16[16,56,128]{2,1,0:T(8,128)(2,1)} %fusion.36), calls=%async_computation.4 | async-start | bytes 458752 | tf_op jit(solution)/shard_map/all_to_all | solution.py:37
  118.9 8.3 %all-to-all-start.5 = ((bf16[4,152,128]{2,1,0:T(8,128)(2,1)}), bf16[4,152,128]{2,1,0:T(8,128)(2,1)S(1)}, u32[]{:S(2)}, u32[]{:S(2)}) async-start(bf16[4,152,128]{2,1,0:T(8,128)(2,1)} %broadcast_in_dim.80), calls=%async_computation.5 | async-start | bytes 311296 | tf_op jit(solution)/shard_map/all_to_all | solution.py:37
  163.8 12.4 %all-to-all-start.6 = ((bf16[16,24,128]{2,1,0:T(8,128)(2,1)}), bf16[16,24,128]{2,1,0:T(8,128)(2,1)S(1)}, u32[]{:S(2)}, u32[]{:S(2)}) async-start(bf16[16,24,128]{2,1,0:T(8,128)(2,1)} %bitcast.189), calls=%async_computation.6 | async-start | bytes 196608 | tf_op jit(solution)/shard_map/all_to_all | solution.py:37
  176.3 12.8 %collective-permute-start = (f32[24,128]{1,0:T(8,128)S(1)}, f32[24,128]{1,0:T(8,128)S(1)}, u32[]{:S(2)}, u32[]{:S(2)}) collective-permute-start(f32[24,128]{1,0:T(8,128)S(1)} %convert_reduce_fusion.2), channel_id=1, source_target_pairs={{0,1},{1,0},{2,3},{3,2},{4,5},{5,4},{6,7},{7,6},{8,9},{9,8},{10,11... | collective-permute-start | bytes 36872 | tf_op jit(solution)/shard_map/ppermute | solution.py:214
  189.8 10.1 %all-to-all-start.7 = ((bf16[16,24,128]{2,1,0:T(8,128)(2,1)}), bf16[16,24,128]{2,1,0:T(8,128)(2,1)S(1)}, u32[]{:S(2)}, u32[]{:S(2)}) async-start(bf16[16,24,128]{2,1,0:T(8,128)(2,1)} %broadcast_in_dim.81), calls=%async_computation.7 | async-start | bytes 196608 | tf_op jit(solution)/shard_map/all_to_all | solution.py:37
  201.9 48.0 %copy-start.8 = (s32[8]{0:T(128)S(1)}, s32[8]{0:T(128)}, u32[]{:S(2)}) copy-start(s32[8]{0:T(128)} %param.41) | copy-start | bytes 100
  201.9 63.6 %copy-start.6 = (f32[8]{0:T(128)S(1)}, f32[8]{0:T(128)}, u32[]{:S(2)}) copy-start(f32[8]{0:T(128)} %param.36) | copy-start | bytes 100
  213.4 5.4 %collective-permute-start.1 = (f32[24,128]{1,0:T(8,128)S(1)}, f32[24,128]{1,0:T(8,128)S(1)}, u32[]{:S(2)}, u32[]{:S(2)}) collective-permute-start(f32[24,128]{1,0:T(8,128)S(1)} %convert_reduce_fusion.1), channel_id=1, source_target_pairs={{0,1},{1,0},{2,3},{3,2},{4,5},{5,4},{6,7},{7,6},{8,9},{9,8},{10,11... | collective-permute-start | bytes 36872 | tf_op jit(solution)/shard_map/ppermute | solution.py:214
  219.4 18.4 %all-to-all-start.9 = ((bf16[16,24,128]{2,1,0:T(8,128)(2,1)}), bf16[16,24,128]{2,1,0:T(8,128)(2,1)S(1)}, u32[]{:S(2)}, u32[]{:S(2)}) async-start(bf16[16,24,128]{2,1,0:T(8,128)(2,1)} %broadcast_in_dim.82), calls=%async_computation.9 | async-start | bytes 196608 | tf_op jit(solution)/shard_map/all_to_all | solution.py:37
  246.4 11.8 %all-to-all-start.11 = ((bf16[4,4,192,128]{3,2,1,0:T(8,128)(2,1)}), bf16[4,4,192,128]{3,2,1,0:T(8,128)(2,1)S(1)}, u32[]{:S(2)}, u32[]{:S(2)}) async-start(bf16[4,4,192,128]{3,2,1,0:T(8,128)(2,1)} %broadcast_in_dim.84), calls=%async_computation.11 | async-start | bytes 1572864 | tf_op jit(solution)/shard_map/all_to_all | solution.py:37
  258.2 10.7 %collective-permute-start.2 = (bf16[4,4,192,128]{3,2,1,0:T(8,128)(2,1)S(1)}, bf16[4,4,192,128]{3,2,1,0:T(8,128)(2,1)}, u32[]{:S(2)}, u32[]{:S(2)}) collective-permute-start(bf16[4,4,192,128]{3,2,1,0:T(8,128)(2,1)S(1)} %all-to-all-done.11), channel_id=1, source_target_pairs={{0,1},{1,0},{2,3},{3,2},{4,5},{5,4},{6,7},{7,6},{8,9},{9,8},{10,11... | collective-permute-start | bytes 2359304 | tf_op jit(solution)/shard_map/ppermute | solution.py:234
  286.7 11.0 %all-to-all-start.12 = ((f32[32,3,128]{2,1,0:T(4,128)}), f32[32,3,128]{2,1,0:T(4,128)S(1)}, u32[]{:S(2)}, u32[]{:S(2)}) async-start(f32[32,3,128]{2,1,0:T(4,128)} %broadcast_in_dim.86), calls=%async_computation.12 | async-start | bytes 131072 | tf_op jit(solution)/shard_map/all_to_all | solution.py:37
  298.4 16.4 %all-to-all-start.13 = ((f32[16,3,128]{2,1,0:T(4,128)}), f32[16,3,128]{2,1,0:T(4,128)S(1)}, u32[]{:S(2)}, u32[]{:S(2)}) async-start(f32[16,3,128]{2,1,0:T(4,128)} %broadcast_in_dim.87), calls=%async_computation.13 | async-start | bytes 65536 | tf_op jit(solution)/shard_map/all_to_all | solution.py:37
Sparse Core Ops, SparseCore 0:
  89.7 72.0 all-gather.1
where the time goes:
time: 325 us; the launch traced here: 323 us
  waiting for transfers between devices  138 us (42%)
  starting transfers between devices  94.6 us (29%)
  local copies, waits for them, and re-layouts  30.7 us (9%)
  blocking collectives  17.3 us (5%)
  matrix products  15.9 us (5%)
  between operations  14.9 us (5%)
  other arithmetic  11.1 us (3%)
    all_to_all x12, waiting for transfers between devices, swap(): return lax.all_to_all(values, axis, 0, 0, tiled=True)  102 us
    all_to_all x12, starting transfers between devices, swap(): return lax.all_to_all(values, axis, 0, 0, tiled=True)  71 us
    all_gather x1, waiting for transfers between devices, on_device(): ffn = lax.all_gather(mine[:, :640], 'z', axis=0, tiled=True)  34.2 us
    all_to_all x2, blocking collectives, swap(): return lax.all_to_all(values, axis, 0, 0, tiled=True)  17.3 us
    ppermute x2, starting transfers between devices, reduce_columns(): return part + lax.ppermute(part, 'c', [(0, 1), (1, 0)])  16.6 us
    convert_element_type x2, local copies, waits for them, and re-layouts, on_device(): wide = full.astype(F32)  10.6 us
    ppermute x1, starting transfers between devices, on_device(): other = lax.ppermute(half, 'c', [(0, 1), (1, 0)])  7.02 us
  transfers between devices with their start and end apart: 16, of which 15 were waited for; matrix products, arithmetic and copies ran while one was open for 5% of the time, Pallas kernels for 0%

commit v1 on v0

--- a/solution.py
+++ b/solution.py
@@ -128,7 +128,9 @@
             )
         )
     mine = swap(jnp.stack(pieces), "y").reshape(128, 1536)
-    ffn = lax.all_gather(mine[:, :640], "z", axis=0, tiled=True)
+    ffn = jnp.concatenate(
+        lax.all_to_all(jnp.stack([mine[:, :640]] * lax.axis_size("z")), "z", 0, 0), axis=0
+    )
     proj = mine[:, 640:1408]
     side = mine[:, 1408:]
     side_wide = side.astype(F32)

time: 325 us -> 397 us (1.22)
  waiting for transfers between devices: 138 us -> 216 us
  between operations: 14.9 us -> 1.68 us
    all_to_all x0 -> x1, waiting for transfers between devices: none -> 113 us  [on_device(): lax.all_to_all(jnp.stack([mine[:, :640]] * lax.axis_size('z')), 'z', 0, 0)]
    all_gather x1 -> x0, waiting for transfers between devices: 34.2 us -> none  [on_device(): ffn = lax.all_gather(mine[:, :640], 'z', axis=0, tiled=True)]
    all_to_all x0 -> x1, starting transfers between devices: none -> 7.54 us  [on_device(): lax.all_to_all(jnp.stack([mine[:, :640]] * lax.axis_size('z')), 'z', 0, 0)]
    ppermute x2, starting transfers between devices: 16.6 us -> 9.47 us  [reduce_columns(): return part + lax.ppermute(part, 'c', [(0, 1), (1, 0)])]
  transfers between devices with their start and end apart: 16 -> 16, of which waited for: 15 -> 15; matrix products, arithmetic and copies ran while one was open for 5% -> 3% of each run, Pallas kernels for 0% -> 0%
where the time goes in v1:
time: 397 us; the launch traced here: 395 us
  waiting for transfers between devices  216 us (54%)
  starting transfers between devices  97.5 us (25%)
  local copies, waits for them, and re-layouts  33.2 us (8%)
  blocking collectives  17.3 us (4%)
  matrix products  16.6 us (4%)
  other arithmetic  13.1 us (3%)
    all_to_all x1, waiting for transfers between devices, on_device(): lax.all_to_all(jnp.stack([mine[:, :640]] * lax.axis_size('z')), 'z', 0, 0)  113 us
    all_to_all x12, waiting for transfers between devices, swap(): return lax.all_to_all(values, axis, 0, 0, tiled=True)  101 us
    all_to_all x12, starting transfers between devices, swap(): return lax.all_to_all(values, axis, 0, 0, tiled=True)  73.5 us
    all_to_all x2, blocking collectives, swap(): return lax.all_to_all(values, axis, 0, 0, tiled=True)  17.3 us
    convert_element_type x2, local copies, waits for them, and re-layouts, on_device(): wide = full.astype(F32)  10.6 us
    ppermute x2, starting transfers between devices, reduce_columns(): return part + lax.ppermute(part, 'c', [(0, 1), (1, 0)])  9.47 us
  transfers between devices with their start and end apart: 16, of which 15 were waited for; matrix products, arithmetic and copies ran while one was open for 3% of the time, Pallas kernels for 0%

profile of v1, /device:TPU:1, one launch (start us, length us, event | category | flops | bytes accessed | tf_op | source)
XLA Modules:
  0.0 395.3 jit_solution(2179890351351210442)
XLA Ops:
  0.7 0.8 convert_bitcast_fusion.10
  1.7 0.7 convert_bitcast_fusion.7
  2.8 0.7 convert_bitcast_fusion.4
  3.8 0.9 fusion.142
  4.7 0.9 fusion.144
  5.6 1.0 fusion.19
  6.8 0.9 fusion.140
  7.8 0.9 concatenate.48
  8.6 0.9 concatenate.49
  9.5 0.9 concatenate.50
  10.3 0.9 concatenate.51
  11.2 0.8 pad_maximum_fusion.1
  12.0 5.0 %all-to-all-start = ((bf16[4,32,1536]{2,1,0:T(8,128)(2,1)}), bf16[4,32,1536]{2,1,0:T(8,128)(2,1)S(1)}, u32[]{:S(2)}, u32[]{:S(2)}) async-start(bf16[4,32,1536]{2,1,0:T(8,128)(2,1)} %pad_maximum_fusion.1), calls=%async_computation | async-start | bytes 786432 | tf_op jit(solution)/shard_map/all_to_all | solution.py:37
  18.0 1.1 fusion.72
  19.5 3.7 all-to-all-done
  23.7 0.7 reshape.548
  24.4 15.5 %all-to-all-start.1 = ((bf16[16,6,896]{2,1,0:T(8,128)(2,1)}), bf16[16,6,896]{2,1,0:T(8,128)(2,1)S(1)}, u32[]{:S(2)}, u32[]{:S(2)}) async-start(bf16[16,6,896]{2,1,0:T(8,128)(2,1)} %reshape.548), calls=%async_computation.1 | async-start | bytes 458752 | tf_op jit(solution)/shard_map/all_to_all | solution.py:37
  40.4 12.2 %all-to-all-done.1 = bf16[16,6,896]{2,1,0:T(8,128)(2,1)S(1)} async-done(((bf16[16,6,896]{2,1,0:T(8,128)(2,1)}), bf16[16,6,896]{2,1,0:T(8,128)(2,1)S(1)}, u32[]{:S(2)}, u32[]{:S(2)}) %all-to-all-start.1) | async-done | bytes 172064 | tf_op jit(solution)/shard_map/all_to_all | solution.py:37
  54.4 8.4 %all-to-all-start.2 = ((bf16[16,8,768]{2,1,0:T(8,128)(2,1)}), bf16[16,8,768]{2,1,0:T(8,128)(2,1)S(1)}, u32[]{:S(2)}, u32[]{:S(2)}) async-start(bf16[16,8,768]{2,1,0:T(8,128)(2,1)} %broadcast_in_dim.72), calls=%async_computation.2 | async-start | bytes 393216 | tf_op jit(solution)/shard_map/all_to_all | solution.py:37
  63.0 12.1 %all-to-all-done.2 = bf16[16,8,768]{2,1,0:T(8,128)(2,1)S(1)} async-done(((bf16[16,8,768]{2,1,0:T(8,128)(2,1)}), bf16[16,8,768]{2,1,0:T(8,128)(2,1)S(1)}, u32[]{:S(2)}, u32[]{:S(2)}) %all-to-all-start.2) | async-done | bytes 196640 | tf_op jit(solution)/shard_map/all_to_all | solution.py:37
  75.2 0.8 broadcast_in_dim.74
  76.1 3.5 all-to-all-start.3
  80.8 6.0 %all-to-all-done.3 = bf16[4,96,768]{2,1,0:T(8,128)(2,1)S(1)} async-done(((bf16[4,96,768]{2,1,0:T(8,128)(2,1)}), bf16[4,96,768]{2,1,0:T(8,128)(2,1)S(1)}, u32[]{:S(2)}, u32[]{:S(2)}) %all-to-all-start.3) | async-done | bytes 589856 | tf_op jit(solution)/shard_map/all_to_all | solution.py:37
  88.5 1.1 select_reduce_fusion
  89.6 1.0 fusion.21
  92.5 7.2 %all-to-all-start.4 = ((bf16[16,56,128]{2,1,0:T(8,128)(2,1)}), bf16[16,56,128]{2,1,0:T(8,128)(2,1)S(1)}, u32[]{:S(2)}, u32[]{:S(2)}) async-start(bf16[16,56,128]{2,1,0:T(8,128)(2,1)} %fusion.36), calls=%async_computation.4 | async-start | bytes 458752 | tf_op jit(solution)/shard_map/all_to_all | solution.py:37
  99.8 12.5 %all-to-all-done.4 = bf16[16,56,128]{2,1,0:T(8,128)(2,1)S(1)} async-done(((bf16[16,56,128]{2,1,0:T(8,128)(2,1)}), bf16[16,56,128]{2,1,0:T(8,128)(2,1)S(1)}, u32[]{:S(2)}, u32[]{:S(2)}) %all-to-all-start.4) | async-done | bytes 229408 | tf_op jit(solution)/shard_map/all_to_all | solution.py:37
  113.5 3.3 all-to-all-start.5
  116.9 4.9 %all-to-all-done.5 = bf16[4,152,128]{2,1,0:T(8,128)(2,1)S(1)} async-done(((bf16[4,152,128]{2,1,0:T(8,128)(2,1)}), bf16[4,152,128]{2,1,0:T(8,128)(2,1)S(1)}, u32[]{:S(2)}, u32[]{:S(2)}) %all-to-all-start.5) | async-done | bytes 155680 | tf_op jit(solution)/shard_map/all_to_all | solution.py:37
  121.8 1.8 stack.102
  123.6 7.5 %all-to-all-start.6 = ((bf16[16,128,640]{2,1,0:T(8,128)(2,1)}), bf16[16,128,640]{2,1,0:T(8,128)(2,1)}, u32[]{:S(2)}, u32[]{:S(2)}) async-start(bf16[16,128,640]{2,1,0:T(8,128)(2,1)} %stack.102), calls=%async_computation.6 | async-start | bytes 5242880 | tf_op jit(solution)/shard_map/all_to_all | solution.py:132
  132.4 113.2 %all-to-all-done.6 = bf16[16,128,640]{2,1,0:T(8,128)(2,1)} async-done(((bf16[16,128,640]{2,1,0:T(8,128)(2,1)}), bf16[16,128,640]{2,1,0:T(8,128)(2,1)}, u32[]{:S(2)}, u32[]{:S(2)}) %all-to-all-start.6) | async-done | bytes 2621472 | tf_op jit(solution)/shard_map/all_to_all | solution.py:132
  245.5 1.4 fusion.17
  247.6 4.8 %all-to-all-start.7 = ((bf16[16,24,128]{2,1,0:T(8,128)(2,1)}), bf16[16,24,128]{2,1,0:T(8,128)(2,1)S(1)}, u32[]{:S(2)}, u32[]{:S(2)}) async-start(bf16[16,24,128]{2,1,0:T(8,128)(2,1)} %bitcast.190), calls=%async_computation.7 | async-start | bytes 196608 | tf_op jit(solution)/shard_map/all_to_all | solution.py:37
  252.6 6.4 %all-to-all-done.7 = bf16[16,24,128]{2,1,0:T(8,128)(2,1)S(1)} async-done(((bf16[16,24,128]{2,1,0:T(8,128)(2,1)}), bf16[16,24,128]{2,1,0:T(8,128)(2,1)S(1)}, u32[]{:S(2)}, u32[]{:S(2)}) %all-to-all-start.7) | async-done | bytes 98336 | tf_op jit(solution)/shard_map/all_to_all | solution.py:37
  259.0 4.8 %collective-permute-start = (f32[24,128]{1,0:T(8,128)S(1)}, f32[24,128]{1,0:T(8,128)S(1)}, u32[]{:S(2)}, u32[]{:S(2)}) collective-permute-start(f32[24,128]{1,0:T(8,128)S(1)} %convert_reduce_fusion.2), channel_id=1, source_target_pairs={{0,1},{1,0},{2,3},{3,2},{4,5},{5,4},{6,7},{7,6},{8,9},{9,8},{10,11... | collective-permute-start | bytes 36872 | tf_op jit(solution)/shard_map/ppermute | solution.py:216
  263.9 0.8 collective-permute-done
  265.3 3.5 all-to-all-start.8
  268.9 6.6 %all-to-all-done.8 = bf16[16,24,128]{2,1,0:T(8,128)(2,1)S(1)} async-done(((bf16[16,24,128]{2,1,0:T(8,128)(2,1)}), bf16[16,24,128]{2,1,0:T(8,128)(2,1)S(1)}, u32[]{:S(2)}, u32[]{:S(2)}) %all-to-all-start.8) | async-done | bytes 98336 | tf_op jit(solution)/shard_map/all_to_all | solution.py:37
  275.6 1.8 fusion.2
  277.4 1.7 fusion.18
  279.1 9.8 %all_to_all.75 = bf16[16,24,128]{2,1,0:T(8,128)(2,1)S(1)} all-to-all(bf16[16,24,128]{2,1,0:T(8,128)(2,1)S(1)} %bitcast.209), channel_id=1, replica_groups=mesh['z'=16,'y'=4,'x'=4,'c'=2] {'y','x'}, dimensions={0} | all-to-all | bytes 196608 | tf_op jit(solution)/shard_map/all_to_all | solution.py:37
  289.0 4.7 %collective-permute-start.1 = (f32[24,128]{1,0:T(8,128)S(1)}, f32[24,128]{1,0:T(8,128)S(1)}, u32[]{:S(2)}, u32[]{:S(2)}) collective-permute-start(f32[24,128]{1,0:T(8,128)S(1)} %convert_reduce_fusion.1), channel_id=1, source_target_pairs={{0,1},{1,0},{2,3},{3,2},{4,5},{5,4},{6,7},{7,6},{8,9},{9,8},{10,11... | collective-permute-start | bytes 36872 | tf_op jit(solution)/shard_map/ppermute | solution.py:216
  293.7 0.8 collective-permute-done.1
  295.2 10.2 %all-to-all-start.10 = ((bf16[16,24,128]{2,1,0:T(8,128)(2,1)}), bf16[16,24,128]{2,1,0:T(8,128)(2,1)S(1)}, u32[]{:S(2)}, u32[]{:S(2)}) async-start(bf16[16,24,128]{2,1,0:T(8,128)(2,1)} %broadcast_in_dim.82), calls=%async_computation.10 | async-start | bytes 196608 | tf_op jit(solution)/shard_map/all_to_all | solution.py:37
  305.3 11.9 %all-to-all-done.10 = bf16[16,24,128]{2,1,0:T(8,128)(2,1)S(1)} async-done(((bf16[16,24,128]{2,1,0:T(8,128)(2,1)}), bf16[16,24,128]{2,1,0:T(8,128)(2,1)S(1)}, u32[]{:S(2)}, u32[]{:S(2)}) %all-to-all-start.10) | async-done | bytes 98336 | tf_op jit(solution)/shard_map/all_to_all | solution.py:37
  317.3 7.5 %all_to_all.76 = bf16[4,192,128]{2,1,0:T(8,128)(2,1)S(1)} all-to-all(bf16[4,192,128]{2,1,0:T(8,128)(2,1)S(1)} %broadcast_in_dim.83), channel_id=1, replica_groups=mesh['z'=16,'y'=4,'x'=4,'c'=2] {'y'}, dimensions={0} | all-to-all | bytes 393216 | tf_op jit(solution)/shard_map/all_to_all | solution.py:37
  324.8 1.0 broadcast_in_dim.84
  325.8 3.5 all-to-all-start.12
  329.4 1.5 gather_fusion
  330.9 6.8 %all-to-all-done.12 = bf16[4,4,192,128]{3,2,1,0:T(8,128)(2,1)S(1)} async-done(((bf16[4,4,192,128]{3,2,1,0:T(8,128)(2,1)}), bf16[4,4,192,128]{3,2,1,0:T(8,128)(2,1)S(1)}, u32[]{:S(2)}, u32[]{:S(2)}) %all-to-all-start.12) | async-done | bytes 786464 | tf_op jit(solution)/shard_map/all_to_all | solution.py:37
  337.7 7.0 %collective-permute-start.2 = (bf16[4,4,192,128]{3,2,1,0:T(8,128)(2,1)S(1)}, bf16[4,4,192,128]{3,2,1,0:T(8,128)(2,1)}, u32[]{:S(2)}, u32[]{:S(2)}) collective-permute-start(bf16[4,4,192,128]{3,2,1,0:T(8,128)(2,1)S(1)} %all-to-all-done.12), channel_id=1, source_target_pairs={{0,1},{1,0},{2,3},{3,2},{4,5},{5,4},{6,7},{7,6},{8,9},{9,8},{10,11... | collective-permute-start | bytes 2359304 | tf_op jit(solution)/shard_map/ppermute | solution.py:236
  345.1 1.7 fusion.6
  346.8 1.6 fusion.7
  348.4 1.2 select_bitcast_fusion.1
  350.1 1.9 convert_bitcast_fusion
  352.1 5.6 %copy.191 = f32[2,192,4,4,128]{4,3,2,1,0:T(4,128)} copy(f32[2,192,4,4,128]{4,1,2,3,0:T(8,128)} %convert_bitcast_fusion) | data formatting | bytes 6291456 | tf_op jit(solution)/shard_map/convert_element_type | solution.py:241
  357.6 5.1 %reshape.577 = f32[384,2048]{1,0:T(8,128)} reshape(f32[2,192,4,4,128]{4,3,2,1,0:T(4,128)} %copy.191) | data formatting | bytes 6291456 | tf_op jit(solution)/shard_map/convert_element_type | solution.py:241
  362.7 2.7 fusion.148
  366.2 3.6 all-to-all-start.13
  369.9 7.3 %all-to-all-done.13 = f32[32,3,128]{2,1,0:T(4,128)S(1)} async-done(((f32[32,3,128]{2,1,0:T(4,128)}), f32[32,3,128]{2,1,0:T(4,128)S(1)}, u32[]{:S(2)}, u32[]{:S(2)}) %all-to-all-start.13) | async-done | bytes 49184 | tf_op jit(solution)/shard_map/all_to_all | solution.py:37
  377.9 4.9 %all-to-all-start.14 = ((f32[16,3,128]{2,1,0:T(4,128)}), f32[16,3,128]{2,1,0:T(4,128)S(1)}, u32[]{:S(2)}, u32[]{:S(2)}) async-start(f32[16,3,128]{2,1,0:T(4,128)} %broadcast_in_dim.87), calls=%async_computation.14 | async-start | bytes 65536 | tf_op jit(solution)/shard_map/all_to_all | solution.py:37
  383.6 10.7 %all-to-all-done.14 = f32[16,3,128]{2,1,0:T(4,128)S(1)} async-done(((f32[16,3,128]{2,1,0:T(4,128)}), f32[16,3,128]{2,1,0:T(4,128)S(1)}, u32[]{:S(2)}, u32[]{:S(2)}) %all-to-all-start.14) | async-done | bytes 24608 | tf_op jit(solution)/shard_map/all_to_all | solution.py:37
  394.4 0.9 copy.196
  (196 shorter events, 18.0 us)
Async XLA Ops:
  0.6 362.1 %copy-start = (bf16[2048,256]{1,0:T(8,128)(2,1)S(1)}, bf16[2048,256]{1,0:T(8,128)(2,1)}, u32[]{:S(2)}) copy-start(bf16[2048,256]{1,0:T(8,128)(2,1)} %param.35) | copy-start | bytes 3145732
  0.6 16.4 %copy-start.18 = (s32[8,48]{1,0:T(8,128)S(1)}, s32[8,48]{1,0:T(8,128)}, u32[]{:S(2)}) copy-start(s32[8,48]{1,0:T(8,128)} %param.40) | copy-start | bytes 4612
  0.7 18.6 %copy-start.14 = (s32[8]{0:T(128)S(1)}, s32[8]{0:T(128)}, u32[]{:S(2)}) copy-start(s32[8]{0:T(128)} %param.39) | copy-start | bytes 100
  11.2 41.9 %copy-start.15 = (f32[128]{0:T(128)S(1)}, f32[128]{0:T(128)}, u32[]{:S(2)}) copy-start(f32[128]{0:T(128)} %param.27) | copy-start | bytes 1540
  11.2 42.2 %copy-start.16 = (f32[128]{0:T(128)S(1)}, f32[128]{0:T(128)}, u32[]{:S(2)}) copy-start(f32[128]{0:T(128)} %param.28) | copy-start | bytes 1540
  12.0 11.2 %all-to-all-start = ((bf16[4,32,1536]{2,1,0:T(8,128)(2,1)}), bf16[4,32,1536]{2,1,0:T(8,128)(2,1)S(1)}, u32[]{:S(2)}, u32[]{:S(2)}) async-start(bf16[4,32,1536]{2,1,0:T(8,128)(2,1)} %pad_maximum_fusion.1), calls=%async_computation | async-start | bytes 786432 | tf_op jit(solution)/shard_map/all_to_all | solution.py:37
  19.4 3.9 copy-start.9
  24.4 28.2 %all-to-all-start.1 = ((bf16[16,6,896]{2,1,0:T(8,128)(2,1)}), bf16[16,6,896]{2,1,0:T(8,128)(2,1)S(1)}, u32[]{:S(2)}, u32[]{:S(2)}) async-start(bf16[16,6,896]{2,1,0:T(8,128)(2,1)} %reshape.548), calls=%async_computation.1 | async-start | bytes 458752 | tf_op jit(solution)/shard_map/all_to_all | solution.py:37
  54.4 20.7 %all-to-all-start.2 = ((bf16[16,8,768]{2,1,0:T(8,128)(2,1)}), bf16[16,8,768]{2,1,0:T(8,128)(2,1)S(1)}, u32[]{:S(2)}, u32[]{:S(2)}) async-start(bf16[16,8,768]{2,1,0:T(8,128)(2,1)} %broadcast_in_dim.72), calls=%async_computation.2 | async-start | bytes 393216 | tf_op jit(solution)/shard_map/all_to_all | solution.py:37
  75.2 13.3 %copy-start.1 = (bf16[8,256,128]{2,1,0:T(8,128)(2,1)S(1)}, bf16[8,256,128]{2,1,0:T(8,128)(2,1)}, u32[]{:S(2)}) copy-start(bf16[8,256,128]{2,1,0:T(8,128)(2,1)} %param.37) | copy-start | bytes 1572868
  76.1 10.7 %all-to-all-start.3 = ((bf16[4,96,768]{2,1,0:T(8,128)(2,1)}), bf16[4,96,768]{2,1,0:T(8,128)(2,1)S(1)}, u32[]{:S(2)}, u32[]{:S(2)}) async-start(bf16[4,96,768]{2,1,0:T(8,128)(2,1)} %broadcast_in_dim.74), calls=%async_computation.3 | async-start | bytes 1179648 | tf_op jit(solution)/shard_map/all_to_all | solution.py:37
  79.5 0.6 copy-start.12
  87.3 3.3 copy-start.3
  88.0 3.1 copy-start.7
  88.1 3.1 copy-start.5
  88.1 2.5 copy-start.11
  92.5 19.8 %all-to-all-start.4 = ((bf16[16,56,128]{2,1,0:T(8,128)(2,1)}), bf16[16,56,128]{2,1,0:T(8,128)(2,1)S(1)}, u32[]{:S(2)}, u32[]{:S(2)}) async-start(bf16[16,56,128]{2,1,0:T(8,128)(2,1)} %fusion.36), calls=%async_computation.4 | async-start | bytes 458752 | tf_op jit(solution)/shard_map/all_to_all | solution.py:37
  113.5 8.3 %all-to-all-start.5 = ((bf16[4,152,128]{2,1,0:T(8,128)(2,1)}), bf16[4,152,128]{2,1,0:T(8,128)(2,1)S(1)}, u32[]{:S(2)}, u32[]{:S(2)}) async-start(bf16[4,152,128]{2,1,0:T(8,128)(2,1)} %broadcast_in_dim.80), calls=%async_computation.5 | async-start | bytes 311296 | tf_op jit(solution)/shard_map/all_to_all | solution.py:37
  123.6 121.9 %all-to-all-start.6 = ((bf16[16,128,640]{2,1,0:T(8,128)(2,1)}), bf16[16,128,640]{2,1,0:T(8,128)(2,1)}, u32[]{:S(2)}, u32[]{:S(2)}) async-start(bf16[16,128,640]{2,1,0:T(8,128)(2,1)} %stack.102), calls=%async_computation.6 | async-start | bytes 5242880 | tf_op jit(solution)/shard_map/all_to_all | solution.py:132
  247.6 11.4 %all-to-all-start.7 = ((bf16[16,24,128]{2,1,0:T(8,128)(2,1)}), bf16[16,24,128]{2,1,0:T(8,128)(2,1)S(1)}, u32[]{:S(2)}, u32[]{:S(2)}) async-start(bf16[16,24,128]{2,1,0:T(8,128)(2,1)} %bitcast.190), calls=%async_computation.7 | async-start | bytes 196608 | tf_op jit(solution)/shard_map/all_to_all | solution.py:37
  259.0 5.6 %collective-permute-start = (f32[24,128]{1,0:T(8,128)S(1)}, f32[24,128]{1,0:T(8,128)S(1)}, u32[]{:S(2)}, u32[]{:S(2)}) collective-permute-start(f32[24,128]{1,0:T(8,128)S(1)} %convert_reduce_fusion.2), channel_id=1, source_target_pairs={{0,1},{1,0},{2,3},{3,2},{4,5},{5,4},{6,7},{7,6},{8,9},{9,8},{10,11... | collective-permute-start | bytes 36872 | tf_op jit(solution)/shard_map/ppermute | solution.py:216
  265.3 10.1 %all-to-all-start.8 = ((bf16[16,24,128]{2,1,0:T(8,128)(2,1)}), bf16[16,24,128]{2,1,0:T(8,128)(2,1)S(1)}, u32[]{:S(2)}, u32[]{:S(2)}) async-start(bf16[16,24,128]{2,1,0:T(8,128)(2,1)} %broadcast_in_dim.81), calls=%async_computation.8 | async-start | bytes 196608 | tf_op jit(solution)/shard_map/all_to_all | solution.py:37
  277.4 52.0 %copy-start.19 = (s32[8]{0:T(128)S(1)}, s32[8]{0:T(128)}, u32[]{:S(2)}) copy-start(s32[8]{0:T(128)} %param.41) | copy-start | bytes 100
  277.4 67.3 %copy-start.10 = (s32[8,48]{1,0:T(8,128)S(1)}, s32[8,48]{1,0:T(8,128)}, u32[]{:S(2)}) copy-start(s32[8,48]{1,0:T(8,128)} %copy-done.9) | copy-start | bytes 4612
  277.4 67.3 %copy-start.13 = (s32[256]{0:T(256)S(1)}, s32[256]{0:T(256)}, u32[]{:S(2)}) copy-start(s32[256]{0:T(256)} %copy-done.12) | copy-start | bytes 3076
  277.4 67.5 %copy-start.17 = (f32[8]{0:T(128)S(1)}, f32[8]{0:T(128)}, u32[]{:S(2)}) copy-start(f32[8]{0:T(128)} %param.36) | copy-start | bytes 100
  277.4 67.7 %copy-start.2 = (bf16[8,256,128]{2,1,0:T(8,128)(2,1)S(1)}, bf16[8,256,128]{2,1,0:T(8,128)(2,1)}, u32[]{:S(2)}) copy-start(bf16[8,256,128]{2,1,0:T(8,128)(2,1)} %param.37) | copy-start | bytes 1572868
  277.4 67.7 %copy-start.8 = (bf16[384,128]{1,0:T(8,128)(2,1)S(1)}, bf16[384,128]{1,0:T(8,128)(2,1)}, u32[]{:S(2)}) copy-start(bf16[384,128]{1,0:T(8,128)(2,1)} %copy-done.7) | copy-start | bytes 294916
  289.0 57.8 %copy-start.4 = (bf16[8,256,128]{2,1,0:T(8,128)(2,1)S(1)}, bf16[8,256,128]{2,1,0:T(8,128)(2,1)}, u32[]{:S(2)}) copy-start(bf16[8,256,128]{2,1,0:T(8,128)(2,1)} %param.38) | copy-start | bytes 1572868
  289.0 57.8 %copy-start.6 = (bf16[384,128]{1,0:T(8,128)(2,1)S(1)}, bf16[384,128]{1,0:T(8,128)(2,1)}, u32[]{:S(2)}) copy-start(bf16[384,128]{1,0:T(8,128)(2,1)} %copy-done.5) | copy-start | bytes 294916
  289.0 5.5 %collective-permute-start.1 = (f32[24,128]{1,0:T(8,128)S(1)}, f32[24,128]{1,0:T(8,128)S(1)}, u32[]{:S(2)}, u32[]{:S(2)}) collective-permute-start(f32[24,128]{1,0:T(8,128)S(1)} %convert_reduce_fusion.1), channel_id=1, source_target_pairs={{0,1},{1,0},{2,3},{3,2},{4,5},{5,4},{6,7},{7,6},{8,9},{9,8},{10,11... | collective-permute-start | bytes 36872 | tf_op jit(solution)/shard_map/ppermute | solution.py:216
  295.2 22.1 %all-to-all-start.10 = ((bf16[16,24,128]{2,1,0:T(8,128)(2,1)}), bf16[16,24,128]{2,1,0:T(8,128)(2,1)S(1)}, u32[]{:S(2)}, u32[]{:S(2)}) async-start(bf16[16,24,128]{2,1,0:T(8,128)(2,1)} %broadcast_in_dim.82), calls=%async_computation.10 | async-start | bytes 196608 | tf_op jit(solution)/shard_map/all_to_all | solution.py:37
  325.8 11.8 %all-to-all-start.12 = ((bf16[4,4,192,128]{3,2,1,0:T(8,128)(2,1)}), bf16[4,4,192,128]{3,2,1,0:T(8,128)(2,1)S(1)}, u32[]{:S(2)}, u32[]{:S(2)}) async-start(bf16[4,4,192,128]{3,2,1,0:T(8,128)(2,1)} %broadcast_in_dim.84), calls=%async_computation.12 | async-start | bytes 1572864 | tf_op jit(solution)/shard_map/all_to_all | solution.py:37
  337.7 10.8 %collective-permute-start.2 = (bf16[4,4,192,128]{3,2,1,0:T(8,128)(2,1)S(1)}, bf16[4,4,192,128]{3,2,1,0:T(8,128)(2,1)}, u32[]{:S(2)}, u32[]{:S(2)}) collective-permute-start(bf16[4,4,192,128]{3,2,1,0:T(8,128)(2,1)S(1)} %all-to-all-done.12), channel_id=1, source_target_pairs={{0,1},{1,0},{2,3},{3,2},{4,5},{5,4},{6,7},{7,6},{8,9},{9,8},{10,11... | collective-permute-start | bytes 2359304 | tf_op jit(solution)/shard_map/ppermute | solution.py:236
  366.2 11.0 %all-to-all-start.13 = ((f32[32,3,128]{2,1,0:T(4,128)}), f32[32,3,128]{2,1,0:T(4,128)S(1)}, u32[]{:S(2)}, u32[]{:S(2)}) async-start(f32[32,3,128]{2,1,0:T(4,128)} %broadcast_in_dim.86), calls=%async_computation.13 | async-start | bytes 131072 | tf_op jit(solution)/shard_map/all_to_all | solution.py:37
  377.9 16.4 %all-to-all-start.14 = ((f32[16,3,128]{2,1,0:T(4,128)}), f32[16,3,128]{2,1,0:T(4,128)S(1)}, u32[]{:S(2)}, u32[]{:S(2)}) async-start(f32[16,3,128]{2,1,0:T(4,128)} %broadcast_in_dim.87), calls=%async_computation.14 | async-start | bytes 65536 | tf_op jit(solution)/shard_map/all_to_all | solution.py:37
